TPU v7x, 32 devices: a whole 2x2x4 slice. The times are simulated.
32 devices in a mesh: gx: 4 (over y, x), gy: 2 (over core), gz: 4 (over z).
Axes of the slice: x: 2, y: 2, z: 4, core: 2. Of those that a mesh axis runs over, the one named last changes fastest.
Arguments:
- load_vector: float32 [32, 32, 2048], P(('gx', 'gy', 'gz')), may hold values from -24 to 24
- matrix_tiles: float32 [512, 7, 128, 128], P(('gx', 'gy', 'gz')), may hold values from -1 to 6, as said below
- tile_cols: int32 [512, 7], P(('gx', 'gy', 'gz')), may hold values from 0 to 15, as said below
- interior_inv: float32 [384, 128, 128], P(('gx', 'gy', 'gz')), may hold values from -0.1 to 0.3, as said below
- schur_inv: float32 [32, 512, 512], P(('gx', 'gy', 'gz')), may hold values from -0.1 to 0.3, as said below
- coarse_basis: float32 [32, 128, 2048], P(('gx', 'gy', 'gz')), may hold values from -0.125 to 0.125
- coarse_inv: float32 [32, 256, 256], P(('gx', 'gy', 'gz')), may hold values from -0.2 to 0.8, as said below
- row_map: int32 [32, 4, 128], P(('gx', 'gy', 'gz')), may hold values from 0 to 127, each once within a row
- face_link: int32 [32, 4], P(('gx', 'gy', 'gz')), may hold values from 0 to 1, as said below
- coarse_id: int32 [32, 4], P(('gx', 'gy', 'gz')), may hold values from 0 to 31, as said below
Outputs:
- solution: float32 [32, 32, 2048], P(('gx', 'gy', 'gz'))
- residual: float32 [32, 32, 2048], P(('gx', 'gy', 'gz'))
Inputs may be any that keep to these rules, and one draw needn't show every extreme that they name: `matrix_tiles`: tile 0 of each block row is its diagonal tile; each subdomain's matrix is symmetric positive definite: the tile of block row i in column block j is the transpose of the tile of block row j in column block i. `tile_cols`: tile 0 of block row i sits in column block i; tiles 1 to 6 sit in column blocks i + a, i - a, i + b, i - b, i + c, i - c modulo 16, for three distinct offsets a, b, c of that subdomain between 1 and (15) // 2; every column block holds exactly 7 tiles. `interior_inv`: each block is symmetric positive definite. `schur_inv`: symmetric positive definite. `coarse_inv`: symmetric positive definite. For partners d and e of round r, entry k of row_map[d, r] and of row_map[e, r] name the same shared unknown. `face_link`: equal for the two partners of a round. coarse_id = owner * 8 + slot, owner being a gz index within the subdomain's line of 4 devices; blocks with the same target are summed. Each subdomain sends at most 2 blocks to one owner and exactly 2 to some owner.
All inputs are finite; a program needn't handle non-finite values.
Results may differ from a plain program's by a relative error of at most 0.00018.
Values sent between devices are 32-bit elements; how exact they have to be, the bound alone decides.
No kernel may reach another device: no remote copies, remote signals or barrier semaphores. Data moves between devices by JAX's collectives and lax.ppermute only.
A program may use at most 64 MiB of HBM per device.

v0:
```python
import jax
import jax.numpy as jnp
from jax import lax
from jax.sharding import PartitionSpec as P

BS = 128
NIN = 12
NRHS = 32
CW = 32
CB = 4
OCAP = 8
ITERS = 2
NB = 16
NL = 2048
HIGH = lax.Precision.HIGHEST


def partner(value, axis, distance):
    return lax.ppermute(value, axis, [(i, i ^ 1 << distance) for i in range(lax.axis_size(axis))])


def on_device(
    load_vector,
    matrix_tiles,
    tile_cols,
    interior_inv,
    schur_inv,
    coarse_basis,
    coarse_inv,
    row_map,
    face_link,
    coarse_id,
):
    load_rows = load_vector[0]
    link_vals = face_link[0]
    face_maps = row_map[0]
    basis_rows = coarse_basis[0]
    schur_mat = schur_inv[0]
    coarse_mat = coarse_inv[0]
    block_ids = coarse_id[0]
    offset = NIN * BS
    line_size = lax.axis_size("gz")
    depth_z = line_size.bit_length() - 1
    depth_y = lax.axis_size("gy").bit_length() - 1
    swap_bits = [0, 1, depth_z, depth_z + depth_y]
    link_float = link_vals.astype(jnp.float32)
    weight = jnp.concatenate(
        [jnp.ones((offset,), jnp.float32)]
        + [jnp.broadcast_to(1.0 - 0.5 * link_float[round_no], (BS,)) for round_no in range(4)]
    )
    lane_ids = jnp.arange(BS, dtype=jnp.int32)
    onehots = [
        (face_maps[round_no][:, None] == lane_ids[None, :]).astype(jnp.float32)
        for round_no in range(4)
    ]

    def assemble(vector):
        outgoing = []
        for round_no in range(4):
            face_rows = vector[:, offset + round_no * BS : offset + (round_no + 1) * BS]
            outgoing.append(jnp.einsum("nj,kj->nk", face_rows, onehots[round_no], precision=HIGH))
        pieces = [vector[:, :offset]]
        for round_no in range(4):
            incoming = partner(outgoing[round_no], ("gx", "gy", "gz"), swap_bits[round_no])
            returned = jnp.dot(incoming, onehots[round_no], precision=HIGH)
            face_rows = vector[:, offset + round_no * BS : offset + (round_no + 1) * BS]
            pieces.append(face_rows + link_float[round_no] * returned)
        return jnp.concatenate(pieces, axis=1)

    group_rows = jnp.arange(line_size * OCAP, dtype=jnp.int32)
    dense_map = (group_rows[:, None] == block_ids[None, :]).astype(jnp.float32)

    def coarse_solve(summed):
        flat_rows = summed.reshape(OCAP * CW, NRHS)
        return jnp.dot(coarse_mat, flat_rows, precision=HIGH).reshape(OCAP, CW * NRHS)

    def coarse_part(contrib):
        summed = lax.psum_scatter(
            jnp.dot(dense_map, contrib, precision=HIGH), "gz", scatter_dimension=0, tiled=True
        )
        solved = coarse_solve(summed)
        all_solved = lax.all_gather(solved, "gz", axis=0, tiled=True)
        return jnp.einsum("ab,ac->bc", dense_map, all_solved, precision=HIGH)

    def precondition(resid):
        scaled = weight * resid
        inner_part = jnp.einsum(
            "bij,nbj->nbi", interior_inv, scaled[:, :offset].reshape(NRHS, NIN, BS), precision=HIGH
        ).reshape(NRHS, offset)
        outer_part = jnp.einsum("ij,nj->ni", schur_mat, scaled[:, offset:], precision=HIGH)
        contrib = jnp.einsum("cl,nl->cn", basis_rows, scaled, precision=HIGH).reshape(CB, CW * NRHS)
        coarse_back = coarse_part(contrib).reshape(CB * CW, NRHS)
        correction = jnp.einsum("cn,cl->nl", coarse_back, basis_rows, precision=HIGH)
        return assemble(weight * (jnp.concatenate([inner_part, outer_part], axis=1) + correction))

    def local_dot(left, right):
        return jnp.sum(weight * left * right, axis=1)

    resid = assemble(load_rows)
    solution = jnp.zeros_like(resid)
    precond_res = precondition(resid)

    def global_rz(left, right):
        return lax.psum(local_dot(left, right), ("gx", "gy", "gz"))

    direction = precond_res
    rho_now = global_rz(resid, precond_res)
    for turn_no in range(ITERS):
        picked = direction.reshape(NRHS, NB, BS)[:, tile_cols]
        product = jnp.einsum("rtij,nrtj->nri", matrix_tiles, picked, precision=HIGH).reshape(
            NRHS, NL
        )
        product_dir = assemble(product)
        curve_sum = lax.psum(local_dot(direction, product_dir), ("gx", "gy", "gz"))
        step_len = (rho_now / curve_sum)[:, None]
        solution = solution + step_len * direction
        resid = resid - step_len * product_dir
        if turn_no + 1 < ITERS:
            precond_res = precondition(resid)
            rho_next = global_rz(resid, precond_res)
            direction = precond_res + (rho_next / rho_now)[:, None] * direction
            rho_now = rho_next
    return (solution[None], resid[None])


def solution(mesh):
    in_specs = (
        P(("gx", "gy", "gz"), None, None),
        P(("gx", "gy", "gz"), None, None, None),
        P(("gx", "gy", "gz"), None),
        P(("gx", "gy", "gz"), None, None),
        P(("gx", "gy", "gz"), None, None),
        P(("gx", "gy", "gz"), None, None),
        P(("gx", "gy", "gz"), None, None),
        P(("gx", "gy", "gz"), None, None),
        P(("gx", "gy", "gz"), None),
        P(("gx", "gy", "gz"), None),
    )
    out_specs = (P(("gx", "gy", "gz"), None, None), P(("gx", "gy", "gz"), None, None))
    return jax.shard_map(
        on_device, mesh=mesh, in_specs=in_specs, out_specs=out_specs, check_vma=False
    )
```

profile of v0, /device:TPU:0, one launch (start us, length us, event | category | flops | bytes accessed | tf_op | source)
XLA Modules:
  0.0 299.2 jit_solution(18162430448153305590)
XLA Ops:
  9.0 3.1 %collective-permute-start = (f32[32,128]{0,1:T(8,128)S(1)}, f32[32,128]{0,1:T(8,128)S(1)}, u32[]{:S(2)}, u32[]{:S(2)}) collective-permute-start(f32[32,128]{0,1:T(8,128)S(1)} %convolution_bitcast_fusion.7), channel_id=1, source_target_pairs={{0,1},{1,0},{2,3},{3,2},{4,5},{5,4},{6,7},{7,6},{8,9},{9,8},{10,11... | collective-permute-start | bytes 49160 | tf_op jit(solution)/shard_map/ppermute | solution.py:19
  13.1 2.7 collective-permute-start.1
  17.7 1.6 collective-permute-start.3
  20.2 1.6 bitcast_dynamic-update-slice_fusion.2
  26.6 1.5 constant_dynamic-update-slice_fusion.4
  28.2 1.7 constant_dynamic-update-slice_fusion.3
  29.9 1.6 constant_dynamic-update-slice_fusion.2
  31.5 2.2 constant_dynamic-update-slice_fusion.1
  35.8 1.5 fusion.97
  41.6 12.3 %reduce-scatter.3.cloned.1.call-done = f32[8,1024]{1,0:T(8,128)} async-done(((f32[32,1024]{1,0:T(8,128)}), f32[8,1024]{1,0:T(8,128)}) %reduce-scatter.3.cloned.1.call-update) | async-done | bytes 32784 | tf_op jit(solution)/shard_map/reduce_scatter | solution.py:78
  55.3 13.4 %all_gather.6 = f32[32,1024]{1,0:T(8,128)S(1)} all-gather(f32[8,1024]{1,0:T(8,128)S(1)} %reshape.579), channel_id=1, replica_groups=mesh['gx'=4,'gy'=2,'gz'=4] {'gz'}, dimensions={0}, use_global_device_ids=true | all-gather | bytes 163840 | tf_op jit(solution)/shard_map/all_gather | solution.py:82
  79.5 9.9 %convolution_bitcast_fusion.1 = f32[16,4,8,128]{3,2,1,0:T(8,128)S(1)} fusion(f32[32,16,7,128]{3,0,2,1:T(8,128)S(1)} %bitcast.200, f32[16,7,128,128]{3,2,1,0:T(8,128)} %param.11), kind=kOutput, calls=%fused_computation.7 | convolution fusion | flops 704643072 | bytes 9437184 | tf_op jit(solution)/shard_map/rtij,nrtj->nri/dot_general | solution.py:110
  91.2 2.0 collective-permute-start.8
  94.0 1.6 collective-permute-start.11
  102.3 39.3 %all-reduce = (f32[32]{0:T(128)S(1)}, f32[32]{0:T(128)S(1)}) all-reduce(f32[32]{0:T(128)S(1)} %get-tuple-element.3, f32[32]{0:T(128)S(1)} %get-tuple-element.2), channel_id=1, replica_groups=mesh['gx'=4,'gy'=2,'gz'=4] {'gx','gy','gz'}, use_global_device_ids=true, to_apply=%region_2.0 | all-reduce | flops 64 | bytes 512 | tf_op jit(solution)/shard_map/psum | solution.py:104
  144.2 1.5 fusion.95
  151.3 14.2 %reduce-scatter.5.cloned.1.call-done = f32[8,1024]{1,0:T(8,128)} async-done(((f32[32,1024]{1,0:T(8,128)}), f32[8,1024]{1,0:T(8,128)}) %reduce-scatter.5.cloned.1.call-update) | async-done | bytes 32784 | tf_op jit(solution)/shard_map/reduce_scatter | solution.py:78
  167.0 13.3 %all_gather.7 = f32[32,1024]{1,0:T(8,128)S(1)} all-gather(f32[8,1024]{1,0:T(8,128)S(1)} %reshape.587), channel_id=1, replica_groups=mesh['gx'=4,'gy'=2,'gz'=4] {'gz'}, dimensions={0}, use_global_device_ids=true | all-gather | bytes 163840 | tf_op jit(solution)/shard_map/all_gather | solution.py:82
  183.6 1.5 collective-permute-start.15
  190.5 40.7 %psum.30 = f32[32]{0:T(128)S(1)} all-reduce(f32[32]{0:T(128)S(1)} %multiply_reduce_fusion.1), channel_id=1, replica_groups=mesh['gx'=4,'gy'=2,'gz'=4] {'gx','gy','gz'}, use_global_device_ids=true, to_apply=%region_7.0 | all-reduce | flops 32 | bytes 256 | tf_op jit(solution)/shard_map/psum | solution.py:104
  232.0 9.9 %convolution_bitcast_fusion = f32[16,4,8,128]{3,2,1,0:T(8,128)S(1)} fusion(f32[32,16,7,128]{3,0,2,1:T(8,128)S(1)} %bitcast.199, f32[16,7,128,128]{3,2,1,0:T(8,128)} %param.11), kind=kOutput, calls=%fused_computation.6 | convolution fusion | flops 704643072 | bytes 9437184 | tf_op jit(solution)/shard_map/rtij,nrtj->nri/dot_general | solution.py:110
  243.2 2.1 collective-permute-start.17
  245.3 2.3 collective-permute-start.19
  251.3 40.0 %psum.31 = f32[32]{0:T(128)S(1)} all-reduce(f32[32]{0:T(128)S(1)} %multiply_reduce_fusion), channel_id=1, replica_groups=mesh['gx'=4,'gy'=2,'gz'=4] {'gx','gy','gz'}, use_global_device_ids=true, to_apply=%region_9.0 | all-reduce | flops 32 | bytes 256 | tf_op jit(solution)/shard_map/psum | solution.py:114
  (222 shorter events, 60.1 us)
Async XLA Ops:
  7.2 46.7 %reduce-scatter.3.cloned.1.call-start = ((), (), s32[]{:S(2)}) async-start(), calls=%async_computation.2 | async-start | bytes 163840 | tf_op jit(solution)/shard_map/reduce_scatter | solution.py:78
  9.0 17.6 %collective-permute-start = (f32[32,128]{0,1:T(8,128)S(1)}, f32[32,128]{0,1:T(8,128)S(1)}, u32[]{:S(2)}, u32[]{:S(2)}) collective-permute-start(f32[32,128]{0,1:T(8,128)S(1)} %convolution_bitcast_fusion.7), channel_id=1, source_target_pairs={{0,1},{1,0},{2,3},{3,2},{4,5},{5,4},{6,7},{7,6},{8,9},{9,8},{10,11... | collective-permute-start | bytes 49160 | tf_op jit(solution)/shard_map/ppermute | solution.py:19
  13.1 15.1 %collective-permute-start.1 = (f32[32,128]{0,1:T(8,128)S(1)}, f32[32,128]{0,1:T(8,128)S(1)}, u32[]{:S(2)}, u32[]{:S(2)}) collective-permute-start(f32[32,128]{0,1:T(8,128)S(1)} %convolution_bitcast_fusion.6), channel_id=1, source_target_pairs={{0,2},{1,3},{2,0},{3,1},{4,6},{5,7},{6,4},{7,5},{8,10},{9,11},{10,... | collective-permute-start | bytes 49160 | tf_op jit(solution)/shard_map/ppermute | solution.py:19
  16.7 13.2 %collective-permute-start.2 = (f32[32,128]{0,1:T(8,128)S(1)}, f32[32,128]{0,1:T(8,128)S(1)}, u32[]{:S(2)}, u32[]{:S(2)}) collective-permute-start(f32[32,128]{0,1:T(8,128)S(1)} %convolution_bitcast_fusion.5), channel_id=1, source_target_pairs={{0,4},{1,5},{2,6},{3,7},{4,0},{5,1},{6,2},{7,3},{8,12},{9,13},{10,... | collective-permute-start | bytes 49160 | tf_op jit(solution)/shard_map/ppermute | solution.py:19
  17.7 13.7 %collective-permute-start.3 = (f32[32,128]{0,1:T(8,128)S(1)}, f32[32,128]{0,1:T(8,128)S(1)}, u32[]{:S(2)}, u32[]{:S(2)}) collective-permute-start(f32[32,128]{0,1:T(8,128)S(1)} %convolution_bitcast_fusion.4), channel_id=1, source_target_pairs={{0,8},{1,9},{2,10},{3,11},{4,12},{5,13},{6,14},{7,15},{8,0},{9,1},... | collective-permute-start | bytes 49160 | tf_op jit(solution)/shard_map/ppermute | solution.py:19
  37.3 128.2 %reduce-scatter.5.cloned.1.call-start = ((), (), s32[]{:S(2)}) async-start(), calls=%async_computation.3 | async-start | bytes 163840 | tf_op jit(solution)/shard_map/reduce_scatter | solution.py:78
  71.2 3.7 %collective-permute-start.4 = (f32[32,128]{1,0:T(8,128)S(1)}, f32[32,128]{1,0:T(8,128)S(1)}, u32[]{:S(2)}, u32[]{:S(2)}) collective-permute-start(f32[32,128]{1,0:T(8,128)S(1)} %fusion.53), channel_id=1, source_target_pairs={{0,1},{1,0},{2,3},{3,2},{4,5},{5,4},{6,7},{7,6},{8,9},{9,8},{10,11... | collective-permute-start | bytes 49160 | tf_op jit(solution)/shard_map/ppermute | solution.py:19
  71.4 4.7 %collective-permute-start.5 = (f32[32,128]{1,0:T(8,128)S(1)}, f32[32,128]{1,0:T(8,128)S(1)}, u32[]{:S(2)}, u32[]{:S(2)}) collective-permute-start(f32[32,128]{1,0:T(8,128)S(1)} %fusion.49), channel_id=1, source_target_pairs={{0,2},{1,3},{2,0},{3,1},{4,6},{5,7},{6,4},{7,5},{8,10},{9,11},{10,... | collective-permute-start | bytes 49160 | tf_op jit(solution)/shard_map/ppermute | solution.py:19
  72.7 4.3 %collective-permute-start.6 = (f32[32,128]{1,0:T(8,128)S(1)}, f32[32,128]{1,0:T(8,128)S(1)}, u32[]{:S(2)}, u32[]{:S(2)}) collective-permute-start(f32[32,128]{1,0:T(8,128)S(1)} %fusion.45), channel_id=1, source_target_pairs={{0,4},{1,5},{2,6},{3,7},{4,0},{5,1},{6,2},{7,3},{8,12},{9,13},{10,... | collective-permute-start | bytes 49160 | tf_op jit(solution)/shard_map/ppermute | solution.py:19
  72.7 5.2 %collective-permute-start.7 = (f32[32,128]{1,0:T(8,128)S(1)}, f32[32,128]{1,0:T(8,128)S(1)}, u32[]{:S(2)}, u32[]{:S(2)}) collective-permute-start(f32[32,128]{1,0:T(8,128)S(1)} %fusion.41), channel_id=1, source_target_pairs={{0,8},{1,9},{2,10},{3,11},{4,12},{5,13},{6,14},{7,15},{8,0},{9,1},... | collective-permute-start | bytes 49160 | tf_op jit(solution)/shard_map/ppermute | solution.py:19
  91.2 6.8 %collective-permute-start.8 = (f32[32,128]{1,0:T(8,128)S(1)}, f32[32,128]{1,0:T(8,128)S(1)}, u32[]{:S(2)}, u32[]{:S(2)}) collective-permute-start(f32[32,128]{1,0:T(8,128)S(1)} %fusion.52), channel_id=1, source_target_pairs={{0,1},{1,0},{2,3},{3,2},{4,5},{5,4},{6,7},{7,6},{8,9},{9,8},{10,11... | collective-permute-start | bytes 49160 | tf_op jit(solution)/shard_map/ppermute | solution.py:19
  93.2 5.6 %collective-permute-start.9 = (f32[32,128]{1,0:T(8,128)S(1)}, f32[32,128]{1,0:T(8,128)S(1)}, u32[]{:S(2)}, u32[]{:S(2)}) collective-permute-start(f32[32,128]{1,0:T(8,128)S(1)} %fusion.48), channel_id=1, source_target_pairs={{0,2},{1,3},{2,0},{3,1},{4,6},{5,7},{6,4},{7,5},{8,10},{9,11},{10,... | collective-permute-start | bytes 49160 | tf_op jit(solution)/shard_map/ppermute | solution.py:19
  94.0 5.7 %collective-permute-start.10 = (f32[32,128]{1,0:T(8,128)S(1)}, f32[32,128]{1,0:T(8,128)S(1)}, u32[]{:S(2)}, u32[]{:S(2)}) collective-permute-start(f32[32,128]{1,0:T(8,128)S(1)} %fusion.44), channel_id=1, source_target_pairs={{0,4},{1,5},{2,6},{3,7},{4,0},{5,1},{6,2},{7,3},{8,12},{9,13},{10,... | collective-permute-start | bytes 49160 | tf_op jit(solution)/shard_map/ppermute | solution.py:19
  94.0 6.7 %collective-permute-start.11 = (f32[32,128]{1,0:T(8,128)S(1)}, f32[32,128]{1,0:T(8,128)S(1)}, u32[]{:S(2)}, u32[]{:S(2)}) collective-permute-start(f32[32,128]{1,0:T(8,128)S(1)} %fusion.40), channel_id=1, source_target_pairs={{0,8},{1,9},{2,10},{3,11},{4,12},{5,13},{6,14},{7,15},{8,0},{9,1},... | collective-permute-start | bytes 49160 | tf_op jit(solution)/shard_map/ppermute | solution.py:19
  180.3 50.8 %copy-start.31 = (f32[32]{0:T(128)S(1)}, f32[32]{0:T(128)}, u32[]{:S(2)}) copy-start(f32[32]{0:T(128)} %copy-done.30) | copy-start | bytes 388
  182.0 3.8 %collective-permute-start.12 = (f32[32,128]{1,0:T(8,128)S(1)}, f32[32,128]{1,0:T(8,128)S(1)}, u32[]{:S(2)}, u32[]{:S(2)}) collective-permute-start(f32[32,128]{1,0:T(8,128)S(1)} %fusion.51), channel_id=1, source_target_pairs={{0,1},{1,0},{2,3},{3,2},{4,5},{5,4},{6,7},{7,6},{8,9},{9,8},{10,11... | collective-permute-start | bytes 49160 | tf_op jit(solution)/shard_map/ppermute | solution.py:19
  182.3 4.7 %collective-permute-start.13 = (f32[32,128]{1,0:T(8,128)S(1)}, f32[32,128]{1,0:T(8,128)S(1)}, u32[]{:S(2)}, u32[]{:S(2)}) collective-permute-start(f32[32,128]{1,0:T(8,128)S(1)} %fusion.47), channel_id=1, source_target_pairs={{0,2},{1,3},{2,0},{3,1},{4,6},{5,7},{6,4},{7,5},{8,10},{9,11},{10,... | collective-permute-start | bytes 49160 | tf_op jit(solution)/shard_map/ppermute | solution.py:19
  183.6 4.3 %collective-permute-start.14 = (f32[32,128]{1,0:T(8,128)S(1)}, f32[32,128]{1,0:T(8,128)S(1)}, u32[]{:S(2)}, u32[]{:S(2)}) collective-permute-start(f32[32,128]{1,0:T(8,128)S(1)} %fusion.43), channel_id=1, source_target_pairs={{0,4},{1,5},{2,6},{3,7},{4,0},{5,1},{6,2},{7,3},{8,12},{9,13},{10,... | collective-permute-start | bytes 49160 | tf_op jit(solution)/shard_map/ppermute | solution.py:19
  183.6 5.2 %collective-permute-start.15 = (f32[32,128]{1,0:T(8,128)S(1)}, f32[32,128]{1,0:T(8,128)S(1)}, u32[]{:S(2)}, u32[]{:S(2)}) collective-permute-start(f32[32,128]{1,0:T(8,128)S(1)} %fusion.39), channel_id=1, source_target_pairs={{0,8},{1,9},{2,10},{3,11},{4,12},{5,13},{6,14},{7,15},{8,0},{9,1},... | collective-permute-start | bytes 49160 | tf_op jit(solution)/shard_map/ppermute | solution.py:19
  242.0 49.3 %copy-start.33 = (f32[32]{0:T(128)S(1)}, f32[32]{0:T(128)}, u32[]{:S(2)}) copy-start(f32[32]{0:T(128)} %copy-done.32) | copy-start | bytes 388
  243.1 4.5 %collective-permute-start.16 = (f32[32,128]{1,0:T(8,128)S(1)}, f32[32,128]{1,0:T(8,128)S(1)}, u32[]{:S(2)}, u32[]{:S(2)}) collective-permute-start(f32[32,128]{1,0:T(8,128)S(1)} %fusion.50), channel_id=1, source_target_pairs={{0,1},{1,0},{2,3},{3,2},{4,5},{5,4},{6,7},{7,6},{8,9},{9,8},{10,11... | collective-permute-start | bytes 49160 | tf_op jit(solution)/shard_map/ppermute | solution.py:19
  243.2 5.2 %collective-permute-start.17 = (f32[32,128]{1,0:T(8,128)S(1)}, f32[32,128]{1,0:T(8,128)S(1)}, u32[]{:S(2)}, u32[]{:S(2)}) collective-permute-start(f32[32,128]{1,0:T(8,128)S(1)} %fusion.46), channel_id=1, source_target_pairs={{0,2},{1,3},{2,0},{3,1},{4,6},{5,7},{6,4},{7,5},{8,10},{9,11},{10,... | collective-permute-start | bytes 49160 | tf_op jit(solution)/shard_map/ppermute | solution.py:19
  245.3 4.0 %collective-permute-start.18 = (f32[32,128]{1,0:T(8,128)S(1)}, f32[32,128]{1,0:T(8,128)S(1)}, u32[]{:S(2)}, u32[]{:S(2)}) collective-permute-start(f32[32,128]{1,0:T(8,128)S(1)} %fusion.42), channel_id=1, source_target_pairs={{0,4},{1,5},{2,6},{3,7},{4,0},{5,1},{6,2},{7,3},{8,12},{9,13},{10,... | collective-permute-start | bytes 49160 | tf_op jit(solution)/shard_map/ppermute | solution.py:19
  245.3 4.9 %collective-permute-start.19 = (f32[32,128]{1,0:T(8,128)S(1)}, f32[32,128]{1,0:T(8,128)S(1)}, u32[]{:S(2)}, u32[]{:S(2)}) collective-permute-start(f32[32,128]{1,0:T(8,128)S(1)} %fusion.38), channel_id=1, source_target_pairs={{0,8},{1,9},{2,10},{3,11},{4,12},{5,13},{6,14},{7,15},{8,0},{9,1},... | collective-permute-start | bytes 49160 | tf_op jit(solution)/shard_map/ppermute | solution.py:19
  (32 other events, 767.2 us)
Sparse Core Ops, SparseCore 0:
  37.4 16.4 reduce-scatter.2
  145.9 19.6 reduce-scatter.4
where the time goes:
time: 300 us; the launch traced here: 299 us
  blocking collectives  147 us (49%)
  matrix products  60.6 us (20%)
  waiting for transfers between devices  28.8 us (10%)
  starting transfers between devices  22 us (7%)
  local copies, waits for them, and re-layouts  20.4 us (7%)
  between operations  17.6 us (6%)
  other arithmetic  3.1 us (1%)
    psum x2, blocking collectives, global_rz(): return lax.psum(local_dot(left, right), ('gx', 'gy', 'gz'))  80 us
    psum x1, blocking collectives, on_device(): curve_sum = lax.psum(local_dot(direction, product_dir), ('gx', 'gy', 'gz'))  40 us
    all_gather x2, blocking collectives, coarse_part(): all_solved = lax.all_gather(solved, 'gz', axis=0, tiled=True)  26.7 us
    reduce_scatter x2, waiting for transfers between devices, coarse_part(): lax.psum_scatter(jnp.dot(dense_map, contrib, precision=HIGH), 'gz', scatt...  26.5 us
    ppermute x20, starting transfers between devices, partner(): lax.ppermute(value, axis, [(i, i ^ 1 << distance) for i in range(lax.axis...  21.9 us
    dot_general x20, matrix products, assemble(): returned = jnp.dot(incoming, onehots[round_no], precision=HIGH)  21 us
    dot_general x2, matrix products, on_device(): jnp.einsum('rtij,nrtj->nri', matrix_tiles, picked, precision=HIGH)  19.8 us
    unnamed x97, local copies, waits for them, and re-layouts  12.5 us
  transfers between devices with their start and end apart: 22, of which 6 were waited for; matrix products, arithmetic and copies ran while one was open for 12% of the time, Pallas kernels for 0%

commit v1 on v0

--- a/solution.py
+++ b/solution.py
@@ -79,7 +79,15 @@
             jnp.dot(dense_map, contrib, precision=HIGH), "gz", scatter_dimension=0, tiled=True
         )
         solved = coarse_solve(summed)
-        all_solved = lax.all_gather(solved, "gz", axis=0, tiled=True)
+        ways, here = (lax.axis_size("gz"), lax.axis_index("gz"))
+        grown, reach = (solved, 1)
+        while reach < ways:
+            theirs = lax.ppermute(grown, "gz", [(d, d ^ reach) for d in range(ways)])
+            mine_first = jnp.concatenate([grown, theirs], axis=0)
+            theirs_first = jnp.concatenate([theirs, grown], axis=0)
+            grown = jnp.where(here & reach == 0, mine_first, theirs_first)
+            reach = 2 * reach
+        all_solved = grown
         return jnp.einsum("ab,ac->bc", dense_map, all_solved, precision=HIGH)
 
     def precondition(resid):

time: 300 us -> 296 us (0.987)
  blocking collectives: 147 us -> 118 us
  waiting for transfers between devices: 28.8 us -> 47.7 us
    all_gather x2 -> x0, blocking collectives: 26.7 us -> none  [coarse_part(): all_solved = lax.all_gather(solved, 'gz', axis=0, tiled=True)]
    ppermute x0 -> x4, waiting for transfers between devices: none -> 13.3 us  [coarse_part(): theirs = lax.ppermute(grown, 'gz', [(d, d ^ reach) for d in range(ways)])]
    reduce_scatter x2, waiting for transfers between devices: 26.5 us -> 30.7 us  [coarse_part(): lax.psum_scatter(jnp.dot(dense_map, contrib, precision=HIGH), 'gz', scatt...]
    unnamed x97 -> x89, local copies, waits for them, and re-layouts: 12.5 us -> 14.3 us
  transfers between devices with their start and end apart: 22 -> 26, of which waited for: 6 -> 10; matrix products, arithmetic and copies ran while one was open for 12% -> 13% of each run, Pallas kernels for 0% -> 0%
where the time goes in v1:
time: 296 us; the launch traced here: 295 us
  blocking collectives  118 us (40%)
  matrix products  62.4 us (21%)
  waiting for transfers between devices  47.7 us (16%)
  starting transfers between devices  22.3 us (8%)
  local copies, waits for them, and re-layouts  22.1 us (7%)
  between operations  17.6 us (6%)
  other arithmetic  4.07 us (1%)
    psum x2, blocking collectives, global_rz(): return lax.psum(local_dot(left, right), ('gx', 'gy', 'gz'))  80.1 us
    psum x1, blocking collectives, on_device(): curve_sum = lax.psum(local_dot(direction, product_dir), ('gx', 'gy', 'gz'))  38.2 us
    reduce_scatter x2, waiting for transfers between devices, coarse_part(): lax.psum_scatter(jnp.dot(dense_map, contrib, precision=HIGH), 'gz', scatt...  30.7 us
    dot_general x20, matrix products, assemble(): returned = jnp.dot(incoming, onehots[round_no], precision=HIGH)  21 us
    ppermute x20, starting transfers between devices, partner(): lax.ppermute(value, axis, [(i, i ^ 1 << distance) for i in range(lax.axis...  20.1 us
    dot_general x2, matrix products, on_device(): jnp.einsum('rtij,nrtj->nri', matrix_tiles, picked, precision=HIGH)  19.8 us
    unnamed x89, local copies, waits for them, and re-layouts  14.3 us
    ppermute x4, waiting for transfers between devices, coarse_part(): theirs = lax.ppermute(grown, 'gz', [(d, d ^ reach) for d in range(ways)])  13.3 us
  transfers between devices with their start and end apart: 26, of which 10 were waited for; matrix products, arithmetic and copies ran while one was open for 13% of the time, Pallas kernels for 0%

profile of v1, /device:TPU:0, one launch (start us, length us, event | category | flops | bytes accessed | tf_op | source)
XLA Modules:
  0.0 294.5 jit_solution(14877393049228928822)
XLA Ops:
  9.0 3.1 %collective-permute-start = (f32[32,128]{0,1:T(8,128)S(1)}, f32[32,128]{0,1:T(8,128)S(1)}, u32[]{:S(2)}, u32[]{:S(2)}) collective-permute-start(f32[32,128]{0,1:T(8,128)S(1)} %convolution_bitcast_fusion.7), channel_id=1, source_target_pairs={{0,1},{1,0},{2,3},{3,2},{4,5},{5,4},{6,7},{7,6},{8,9},{9,8},{10,11... | collective-permute-start | bytes 49160 | tf_op jit(solution)/shard_map/ppermute | solution.py:19
  13.1 2.7 collective-permute-start.1
  17.7 1.6 collective-permute-start.3
  20.2 1.6 bitcast_dynamic-update-slice_fusion.2
  26.7 1.5 constant_dynamic-update-slice_fusion.4
  28.2 1.7 constant_dynamic-update-slice_fusion.3
  29.9 1.6 constant_dynamic-update-slice_fusion.2
  31.5 2.2 constant_dynamic-update-slice_fusion.1
  38.9 14.3 %reduce-scatter.3.cloned.1.call-done = f32[8,1024]{1,0:T(8,128)} async-done(((f32[32,1024]{1,0:T(8,128)}), f32[8,1024]{1,0:T(8,128)}) %reduce-scatter.3.cloned.1.call-update) | async-done | bytes 32784 | tf_op jit(solution)/shard_map/reduce_scatter | solution.py:78
  56.3 3.3 %collective-permute-done.4 = f32[8,1024]{1,0:T(8,128)S(1)} collective-permute-done((f32[8,1024]{1,0:T(8,128)S(1)}, f32[8,1024]{1,0:T(8,128)S(1)}, u32[]{:S(2)}, u32[]{:S(2)}) %collective-permute-start.4) | collective-permute-done | bytes 32800 | tf_op jit(solution)/shard_map/ppermute | solution.py:85
  62.0 3.3 %collective-permute-done.5 = f32[16,1024]{1,0:T(8,128)S(1)} collective-permute-done((f32[16,1024]{1,0:T(8,128)S(1)}, f32[16,1024]{1,0:T(8,128)S(1)}, u32[]{:S(2)}, u32[]{:S(2)}) %collective-permute-start.5) | collective-permute-done | bytes 65568 | tf_op jit(solution)/shard_map/ppermute | solution.py:85
  76.1 9.9 %convolution_bitcast_fusion.1 = f32[16,4,8,128]{3,2,1,0:T(8,128)S(1)} fusion(f32[32,16,7,128]{3,0,2,1:T(8,128)S(1)} %bitcast.198, f32[16,7,128,128]{3,2,1,0:T(8,128)} %param.11), kind=kOutput, calls=%fused_computation.7 | convolution fusion | flops 704643072 | bytes 9437184 | tf_op jit(solution)/shard_map/rtij,nrtj->nri/dot_general | solution.py:118
  87.8 2.0 collective-permute-start.10
  98.6 39.5 %all-reduce = (f32[32]{0:T(128)S(1)}, f32[32]{0:T(128)S(1)}) all-reduce(f32[32]{0:T(128)S(1)} %get-tuple-element.3, f32[32]{0:T(128)S(1)} %get-tuple-element.2), channel_id=1, replica_groups=mesh['gx'=4,'gy'=2,'gz'=4] {'gx','gy','gz'}, use_global_device_ids=true, to_apply=%region_2.3 | all-reduce | flops 64 | bytes 512 | tf_op jit(solution)/shard_map/psum | solution.py:112
  145.8 16.4 %reduce-scatter.5.cloned.1.call-done = f32[8,1024]{1,0:T(8,128)} async-done(((f32[32,1024]{1,0:T(8,128)}), f32[8,1024]{1,0:T(8,128)}) %reduce-scatter.5.cloned.1.call-update) | async-done | bytes 32784 | tf_op jit(solution)/shard_map/reduce_scatter | solution.py:78
  165.2 3.3 %collective-permute-done.14 = f32[8,1024]{1,0:T(8,128)S(1)} collective-permute-done((f32[8,1024]{1,0:T(8,128)S(1)}, f32[8,1024]{1,0:T(8,128)S(1)}, u32[]{:S(2)}, u32[]{:S(2)}) %collective-permute-start.14) | collective-permute-done | bytes 32800 | tf_op jit(solution)/shard_map/ppermute | solution.py:85
  170.8 3.4 %collective-permute-done.15 = f32[16,1024]{1,0:T(8,128)S(1)} collective-permute-done((f32[16,1024]{1,0:T(8,128)S(1)}, f32[16,1024]{1,0:T(8,128)S(1)}, u32[]{:S(2)}, u32[]{:S(2)}) %collective-permute-start.15) | collective-permute-done | bytes 65568 | tf_op jit(solution)/shard_map/ppermute | solution.py:85
  176.9 1.5 collective-permute-start.19
  184.4 40.6 %psum.30 = f32[32]{0:T(128)S(1)} all-reduce(f32[32]{0:T(128)S(1)} %multiply_reduce_fusion.1), channel_id=1, replica_groups=mesh['gx'=4,'gy'=2,'gz'=4] {'gx','gy','gz'}, use_global_device_ids=true, to_apply=%region_7.8 | all-reduce | flops 32 | bytes 256 | tf_op jit(solution)/shard_map/psum | solution.py:112
  225.9 9.9 %convolution_bitcast_fusion = f32[16,4,8,128]{3,2,1,0:T(8,128)S(1)} fusion(f32[32,16,7,128]{3,0,2,1:T(8,128)S(1)} %bitcast.197, f32[16,7,128,128]{3,2,1,0:T(8,128)} %param.11), kind=kOutput, calls=%fused_computation.6 | convolution fusion | flops 704643072 | bytes 9437184 | tf_op jit(solution)/shard_map/rtij,nrtj->nri/dot_general | solution.py:118
  236.9 2.1 collective-permute-start.21
  239.1 2.3 collective-permute-start.23
  247.5 38.2 %psum.31 = f32[32]{0:T(128)S(1)} all-reduce(f32[32]{0:T(128)S(1)} %multiply_reduce_fusion), channel_id=1, replica_groups=mesh['gx'=4,'gy'=2,'gz'=4] {'gx','gy','gz'}, use_global_device_ids=true, to_apply=%region_9.10 | all-reduce | flops 32 | bytes 256 | tf_op jit(solution)/shard_map/psum | solution.py:122
  285.8 1.9 multiply_subtract_fusion
  (222 shorter events, 69.0 us)
Async XLA Ops:
  7.2 46.1 %reduce-scatter.3.cloned.1.call-start = ((), (), s32[]{:S(2)}) async-start(), calls=%async_computation.2 | async-start | bytes 163840 | tf_op jit(solution)/shard_map/reduce_scatter | solution.py:78
  9.0 17.6 %collective-permute-start = (f32[32,128]{0,1:T(8,128)S(1)}, f32[32,128]{0,1:T(8,128)S(1)}, u32[]{:S(2)}, u32[]{:S(2)}) collective-permute-start(f32[32,128]{0,1:T(8,128)S(1)} %convolution_bitcast_fusion.7), channel_id=1, source_target_pairs={{0,1},{1,0},{2,3},{3,2},{4,5},{5,4},{6,7},{7,6},{8,9},{9,8},{10,11... | collective-permute-start | bytes 49160 | tf_op jit(solution)/shard_map/ppermute | solution.py:19
  13.1 15.1 %collective-permute-start.1 = (f32[32,128]{0,1:T(8,128)S(1)}, f32[32,128]{0,1:T(8,128)S(1)}, u32[]{:S(2)}, u32[]{:S(2)}) collective-permute-start(f32[32,128]{0,1:T(8,128)S(1)} %convolution_bitcast_fusion.6), channel_id=1, source_target_pairs={{0,2},{1,3},{2,0},{3,1},{4,6},{5,7},{6,4},{7,5},{8,10},{9,11},{10,... | collective-permute-start | bytes 49160 | tf_op jit(solution)/shard_map/ppermute | solution.py:19
  16.7 13.2 %collective-permute-start.2 = (f32[32,128]{0,1:T(8,128)S(1)}, f32[32,128]{0,1:T(8,128)S(1)}, u32[]{:S(2)}, u32[]{:S(2)}) collective-permute-start(f32[32,128]{0,1:T(8,128)S(1)} %convolution_bitcast_fusion.5), channel_id=1, source_target_pairs={{0,4},{1,5},{2,6},{3,7},{4,0},{5,1},{6,2},{7,3},{8,12},{9,13},{10,... | collective-permute-start | bytes 49160 | tf_op jit(solution)/shard_map/ppermute | solution.py:19
  17.7 13.8 %collective-permute-start.3 = (f32[32,128]{0,1:T(8,128)S(1)}, f32[32,128]{0,1:T(8,128)S(1)}, u32[]{:S(2)}, u32[]{:S(2)}) collective-permute-start(f32[32,128]{0,1:T(8,128)S(1)} %convolution_bitcast_fusion.4), channel_id=1, source_target_pairs={{0,8},{1,9},{2,10},{3,11},{4,12},{5,13},{6,14},{7,15},{8,0},{9,1},... | collective-permute-start | bytes 49160 | tf_op jit(solution)/shard_map/ppermute | solution.py:19
  36.6 125.5 %reduce-scatter.5.cloned.1.call-start = ((), (), s32[]{:S(2)}) async-start(), calls=%async_computation.3 | async-start | bytes 163840 | tf_op jit(solution)/shard_map/reduce_scatter | solution.py:78
  55.6 4.0 %collective-permute-start.4 = (f32[8,1024]{1,0:T(8,128)S(1)}, f32[8,1024]{1,0:T(8,128)S(1)}, u32[]{:S(2)}, u32[]{:S(2)}) collective-permute-start(f32[8,1024]{1,0:T(8,128)S(1)} %reshape.579), channel_id=1, source_target_pairs={{0,1},{1,0},{2,3},{3,2},{4,5},{5,4},{6,7},{7,6},{8,9},{9,8},{10,11... | collective-permute-start | bytes 98312 | tf_op jit(solution)/shard_map/ppermute | solution.py:85
  59.7 5.7 %collective-permute-start.5 = (f32[16,1024]{1,0:T(8,128)S(1)}, f32[16,1024]{1,0:T(8,128)S(1)}, u32[]{:S(2)}, u32[]{:S(2)}) collective-permute-start(f32[16,1024]{1,0:T(8,128)S(1)} %maximum_select_fusion.4), channel_id=1, source_target_pairs={{0,2},{1,3},{2,0},{3,1},{4,6},{5,7},{6,4},{7,5},{8,10},{9,11},{10,... | collective-permute-start | bytes 196616 | tf_op jit(solution)/shard_map/ppermute | solution.py:85
  68.0 4.7 %collective-permute-start.7 = (f32[32,128]{1,0:T(8,128)S(1)}, f32[32,128]{1,0:T(8,128)S(1)}, u32[]{:S(2)}, u32[]{:S(2)}) collective-permute-start(f32[32,128]{1,0:T(8,128)S(1)} %fusion.61), channel_id=1, source_target_pairs={{0,2},{1,3},{2,0},{3,1},{4,6},{5,7},{6,4},{7,5},{8,10},{9,11},{10,... | collective-permute-start | bytes 49160 | tf_op jit(solution)/shard_map/ppermute | solution.py:19
  68.6 5.0 %collective-permute-start.8 = (f32[32,128]{1,0:T(8,128)S(1)}, f32[32,128]{1,0:T(8,128)S(1)}, u32[]{:S(2)}, u32[]{:S(2)}) collective-permute-start(f32[32,128]{1,0:T(8,128)S(1)} %fusion.57), channel_id=1, source_target_pairs={{0,4},{1,5},{2,6},{3,7},{4,0},{5,1},{6,2},{7,3},{8,12},{9,13},{10,... | collective-permute-start | bytes 49160 | tf_op jit(solution)/shard_map/ppermute | solution.py:19
  68.6 5.8 %collective-permute-start.9 = (f32[32,128]{1,0:T(8,128)S(1)}, f32[32,128]{1,0:T(8,128)S(1)}, u32[]{:S(2)}, u32[]{:S(2)}) collective-permute-start(f32[32,128]{1,0:T(8,128)S(1)} %fusion.53), channel_id=1, source_target_pairs={{0,8},{1,9},{2,10},{3,11},{4,12},{5,13},{6,14},{7,15},{8,0},{9,1},... | collective-permute-start | bytes 49160 | tf_op jit(solution)/shard_map/ppermute | solution.py:19
  87.8 6.4 %collective-permute-start.10 = (f32[32,128]{1,0:T(8,128)S(1)}, f32[32,128]{1,0:T(8,128)S(1)}, u32[]{:S(2)}, u32[]{:S(2)}) collective-permute-start(f32[32,128]{1,0:T(8,128)S(1)} %fusion.64), channel_id=1, source_target_pairs={{0,1},{1,0},{2,3},{3,2},{4,5},{5,4},{6,7},{7,6},{8,9},{9,8},{10,11... | collective-permute-start | bytes 49160 | tf_op jit(solution)/shard_map/ppermute | solution.py:19
  89.9 5.2 %collective-permute-start.11 = (f32[32,128]{1,0:T(8,128)S(1)}, f32[32,128]{1,0:T(8,128)S(1)}, u32[]{:S(2)}, u32[]{:S(2)}) collective-permute-start(f32[32,128]{1,0:T(8,128)S(1)} %fusion.60), channel_id=1, source_target_pairs={{0,2},{1,3},{2,0},{3,1},{4,6},{5,7},{6,4},{7,5},{8,10},{9,11},{10,... | collective-permute-start | bytes 49160 | tf_op jit(solution)/shard_map/ppermute | solution.py:19
  90.4 5.7 %collective-permute-start.12 = (f32[32,128]{1,0:T(8,128)S(1)}, f32[32,128]{1,0:T(8,128)S(1)}, u32[]{:S(2)}, u32[]{:S(2)}) collective-permute-start(f32[32,128]{1,0:T(8,128)S(1)} %fusion.56), channel_id=1, source_target_pairs={{0,4},{1,5},{2,6},{3,7},{4,0},{5,1},{6,2},{7,3},{8,12},{9,13},{10,... | collective-permute-start | bytes 49160 | tf_op jit(solution)/shard_map/ppermute | solution.py:19
  90.4 7.1 %collective-permute-start.13 = (f32[32,128]{1,0:T(8,128)S(1)}, f32[32,128]{1,0:T(8,128)S(1)}, u32[]{:S(2)}, u32[]{:S(2)}) collective-permute-start(f32[32,128]{1,0:T(8,128)S(1)} %fusion.52), channel_id=1, source_target_pairs={{0,8},{1,9},{2,10},{3,11},{4,12},{5,13},{6,14},{7,15},{8,0},{9,1},... | collective-permute-start | bytes 49160 | tf_op jit(solution)/shard_map/ppermute | solution.py:19
  164.5 4.0 %collective-permute-start.14 = (f32[8,1024]{1,0:T(8,128)S(1)}, f32[8,1024]{1,0:T(8,128)S(1)}, u32[]{:S(2)}, u32[]{:S(2)}) collective-permute-start(f32[8,1024]{1,0:T(8,128)S(1)} %reshape.587), channel_id=1, source_target_pairs={{0,1},{1,0},{2,3},{3,2},{4,5},{5,4},{6,7},{7,6},{8,9},{9,8},{10,11... | collective-permute-start | bytes 98312 | tf_op jit(solution)/shard_map/ppermute | solution.py:85
  168.5 5.7 %collective-permute-start.15 = (f32[16,1024]{1,0:T(8,128)S(1)}, f32[16,1024]{1,0:T(8,128)S(1)}, u32[]{:S(2)}, u32[]{:S(2)}) collective-permute-start(f32[16,1024]{1,0:T(8,128)S(1)} %maximum_select_fusion.5), channel_id=1, source_target_pairs={{0,2},{1,3},{2,0},{3,1},{4,6},{5,7},{6,4},{7,5},{8,10},{9,11},{10,... | collective-permute-start | bytes 196616 | tf_op jit(solution)/shard_map/ppermute | solution.py:85
  176.2 4.7 %collective-permute-start.17 = (f32[32,128]{1,0:T(8,128)S(1)}, f32[32,128]{1,0:T(8,128)S(1)}, u32[]{:S(2)}, u32[]{:S(2)}) collective-permute-start(f32[32,128]{1,0:T(8,128)S(1)} %fusion.59), channel_id=1, source_target_pairs={{0,2},{1,3},{2,0},{3,1},{4,6},{5,7},{6,4},{7,5},{8,10},{9,11},{10,... | collective-permute-start | bytes 49160 | tf_op jit(solution)/shard_map/ppermute | solution.py:19
  176.9 5.0 %collective-permute-start.18 = (f32[32,128]{1,0:T(8,128)S(1)}, f32[32,128]{1,0:T(8,128)S(1)}, u32[]{:S(2)}, u32[]{:S(2)}) collective-permute-start(f32[32,128]{1,0:T(8,128)S(1)} %fusion.55), channel_id=1, source_target_pairs={{0,4},{1,5},{2,6},{3,7},{4,0},{5,1},{6,2},{7,3},{8,12},{9,13},{10,... | collective-permute-start | bytes 49160 | tf_op jit(solution)/shard_map/ppermute | solution.py:19
  176.9 5.8 %collective-permute-start.19 = (f32[32,128]{1,0:T(8,128)S(1)}, f32[32,128]{1,0:T(8,128)S(1)}, u32[]{:S(2)}, u32[]{:S(2)}) collective-permute-start(f32[32,128]{1,0:T(8,128)S(1)} %fusion.51), channel_id=1, source_target_pairs={{0,8},{1,9},{2,10},{3,11},{4,12},{5,13},{6,14},{7,15},{8,0},{9,1},... | collective-permute-start | bytes 49160 | tf_op jit(solution)/shard_map/ppermute | solution.py:19
  236.9 6.3 %collective-permute-start.20 = (f32[32,128]{1,0:T(8,128)S(1)}, f32[32,128]{1,0:T(8,128)S(1)}, u32[]{:S(2)}, u32[]{:S(2)}) collective-permute-start(f32[32,128]{1,0:T(8,128)S(1)} %fusion.62), channel_id=1, source_target_pairs={{0,1},{1,0},{2,3},{3,2},{4,5},{5,4},{6,7},{7,6},{8,9},{9,8},{10,11... | collective-permute-start | bytes 49160 | tf_op jit(solution)/shard_map/ppermute | solution.py:19
  236.9 7.0 %collective-permute-start.21 = (f32[32,128]{1,0:T(8,128)S(1)}, f32[32,128]{1,0:T(8,128)S(1)}, u32[]{:S(2)}, u32[]{:S(2)}) collective-permute-start(f32[32,128]{1,0:T(8,128)S(1)} %fusion.58), channel_id=1, source_target_pairs={{0,2},{1,3},{2,0},{3,1},{4,6},{5,7},{6,4},{7,5},{8,10},{9,11},{10,... | collective-permute-start | bytes 49160 | tf_op jit(solution)/shard_map/ppermute | solution.py:19
  239.1 5.8 %collective-permute-start.22 = (f32[32,128]{1,0:T(8,128)S(1)}, f32[32,128]{1,0:T(8,128)S(1)}, u32[]{:S(2)}, u32[]{:S(2)}) collective-permute-start(f32[32,128]{1,0:T(8,128)S(1)} %fusion.54), channel_id=1, source_target_pairs={{0,4},{1,5},{2,6},{3,7},{4,0},{5,1},{6,2},{7,3},{8,12},{9,13},{10,... | collective-permute-start | bytes 49160 | tf_op jit(solution)/shard_map/ppermute | solution.py:19
  239.1 6.7 %collective-permute-start.23 = (f32[32,128]{1,0:T(8,128)S(1)}, f32[32,128]{1,0:T(8,128)S(1)}, u32[]{:S(2)}, u32[]{:S(2)}) collective-permute-start(f32[32,128]{1,0:T(8,128)S(1)} %fusion.50), channel_id=1, source_target_pairs={{0,8},{1,9},{2,10},{3,11},{4,12},{5,13},{6,14},{7,15},{8,0},{9,1},... | collective-permute-start | bytes 49160 | tf_op jit(solution)/shard_map/ppermute | solution.py:19
  (32 other events, 735.8 us)
Sparse Core Ops, SparseCore 0:
  36.7 16.4 reduce-scatter.2
  142.3 19.8 reduce-scatter.4
